TPU v7x, 128 devices: a whole 4x4x4 slice. The times are simulated.
128 devices in a mesh: dp: 16 (over y, z), sub: 8 (over x, core).
Axes of the slice: x: 4, y: 4, z: 4, core: 2. Of those that a mesh axis runs over, the one named last changes fastest.
Arguments:
- queries: bfloat16 [64, 64, 576], P('dp'), may hold values from -195 to 195
- own_cache: bfloat16 [64, 2048, 576], P('dp', 'sub'), may hold values from -8 to 8
- own_len: int32 [64, 8], P('dp', 'sub'), may hold values from 2 to 256
- host_cache: bfloat16 [16, 8, 16, 1024, 576], P('dp', 'sub'), may hold values from -8 to 8
- host_len: int32 [16, 8, 16], P('dp', 'sub'), may hold values from 2 to 1024
- page_plan: int32 [16, 8, 16], P('dp', 'sub'), may hold values from 0 to 3
- value_up: bfloat16 [64, 512, 128], P('sub'), may hold values from -0.25 to 0.25
Outputs:
- attended: bfloat16 [64, 64, 128], P('dp', 'sub')
All inputs are finite; a program needn't handle non-finite values.
Results may differ from a plain program's by a relative error of at most 0.008.
Values may be sent and summed in bfloat16 or wider, within the bound.
A program may use at most 128 MiB of HBM per device.

v0:
```python
import jax
import jax.numpy as jnp
from jax import lax
from jax.sharding import PartitionSpec as P

DL = 512


score_scale = 192 ** (-0.5)
masked_score = -1e30


def side_by_side(arrays, axis, split_dim, concat_dim, along):
    columns = [a.reshape(*a.shape[:along], -1) for a in arrays]
    both = jnp.concatenate(columns, axis=along)
    result, at, finished = (
        lax.all_to_all(both, axis, split_axis=split_dim, concat_axis=concat_dim, tiled=True),
        0,
        [],
    )
    for a, column in zip(arrays, columns):
        section = result[..., at : at + column.shape[along]]
        finished.append(section.reshape(*section.shape[:along], *a.shape[along:]))
        at += column.shape[along]
    return tuple(finished)


def attend(queries, slot_cache, lengths):
    scores = (
        jnp.einsum("phd,ptd->pht", queries, slot_cache, preferred_element_type=jnp.float32)
        * score_scale
    )
    position = lax.broadcasted_iota(jnp.int32, (1, 1, slot_cache.shape[1]), 2)
    scores = jnp.where(position < lengths[:, None, None], scores, masked_score)
    largest = jnp.max(scores, axis=2, keepdims=True)
    exponent = jnp.exp(scores - largest)
    totals = jnp.sum(exponent, axis=2)
    weights = exponent.astype(jnp.bfloat16)
    weighted = jnp.einsum(
        "pht,ptd->phd", weights, slot_cache[:, :, :DL], preferred_element_type=jnp.float32
    )
    return (weighted / totals[:, :, None], largest[:, :, 0] + jnp.log(totals))


def combine_group(device_out, device_lse):
    pieces_out, pieces_lse = side_by_side((device_out[None], device_lse[None]), "sub", 2, 0, 3)
    piece_peak = jnp.max(pieces_lse, axis=0)
    piece_weight = jnp.exp(pieces_lse - piece_peak[None])
    weight_total = jnp.sum(piece_weight, axis=0)
    share_out = jnp.sum(piece_weight[..., None] * pieces_out, axis=0) / weight_total[..., None]
    share_lse = piece_peak + jnp.log(weight_total)
    return (share_out, share_lse)


def local(queries, own_cache, own_len, host_cache, host_len, page_plan, value_up):
    groups = lax.axis_size("dp")
    request_count, head_count, width = queries.shape
    targets = page_plan.reshape(groups)
    matched = targets[:, None] == lax.broadcasted_iota(jnp.int32, (groups, request_count), 1)
    onehot_table = matched.astype(jnp.bfloat16)
    outgoing = jnp.dot(
        onehot_table,
        queries.reshape(request_count, head_count * width),
        preferred_element_type=jnp.float32,
    )
    outgoing = outgoing.astype(jnp.bfloat16).reshape(groups, head_count, width)
    slot_cache = host_cache.reshape(groups, host_cache.shape[3], width)
    slot_lengths = host_len.reshape(groups)
    helper_out, helper_lse = attend(
        lax.all_to_all(outgoing, "dp", split_axis=0, concat_axis=0, tiled=True),
        slot_cache,
        slot_lengths,
    )
    back_out = lax.all_to_all(helper_out, "dp", split_axis=0, concat_axis=0, tiled=True)
    back_lse = lax.all_to_all(helper_lse, "dp", split_axis=0, concat_axis=0, tiled=True)
    own_out, own_lse = attend(queries, own_cache, own_len.reshape(request_count))
    masked = jnp.where(matched[:, :, None], back_lse[:, None, :], masked_score)
    largest = jnp.maximum(own_lse, jnp.max(masked, axis=0))
    own_weight = jnp.exp(own_lse - largest)
    help_weight = jnp.exp(masked - largest[None])
    gathered = jnp.einsum("pch,phd->chd", help_weight, back_out)
    totals = own_weight + jnp.sum(help_weight, axis=0)
    device_out = (own_weight[..., None] * own_out + gathered) / totals[..., None]
    device_lse = largest + jnp.log(totals)
    latent, unused_lse = combine_group(device_out, device_lse)
    latent = latent.astype(jnp.bfloat16)
    result = jnp.einsum("chd,hde->che", latent, value_up, preferred_element_type=jnp.float32)
    return result.astype(jnp.bfloat16)


def solution(mesh):
    return jax.shard_map(
        local,
        mesh=mesh,
        in_specs=(
            P("dp", None, None),
            P("dp", "sub", None),
            P("dp", "sub"),
            P("dp", "sub", None, None, None),
            P("dp", "sub", None),
            P("dp", "sub", None),
            P("sub", None, None),
        ),
        out_specs=P("dp", "sub", None),
        check_vma=False,
    )
```

profile of v0, /device:TPU:1, one launch (start us, length us, event | category | flops | bytes accessed | tf_op | source)
XLA Modules:
  0.0 117.4 jit_solution(11779728282394794927)
XLA Ops:
  0.0 1.5 %reshape.178 = bf16[4,36864]{1,0:T(4,128)(2,1)S(1)} reshape(bf16[4,64,576]{2,1,0:T(8,128)(2,1)} %param.7) | data formatting | bytes 589824 | tf_op jit(solution)/shard_map/reshape | solution.py:63
  1.5 1.2 %convolution_convert_fusion = bf16[16,36864]{1,0:T(8,128)(2,1)S(1)} fusion(bf16[4,36864]{1,0:T(4,128)(2,1)S(1)} %reshape.178, s32[16]{0:T(128)} %bitcast.53), kind=kOutput, calls=%fused_computation | convolution fusion | flops 5308480 | bytes 1474624 | tf_op jit(solution)/shard_map/dot_general | solution.py:61
  2.7 2.5 %reshape.179 = bf16[16,64,576]{2,1,0:T(8,128)(2,1)} reshape(bf16[16,36864]{1,0:T(8,128)(2,1)S(1)} %convolution_convert_fusion) | data formatting | bytes 2359296 | tf_op jit(solution)/shard_map/reshape | solution.py:66
  5.2 8.6 %all-to-all-start = ((bf16[16,64,576]{2,1,0:T(8,128)(2,1)}), bf16[16,64,576]{2,1,0:T(8,128)(2,1)S(1)}, u32[]{:S(2)}, u32[]{:S(2)}) async-start(bf16[16,64,576]{2,1,0:T(8,128)(2,1)} %reshape.179), calls=%async_computation | async-start | bytes 2621440 | tf_op jit(solution)/shard_map/all_to_all | solution.py:70
  13.8 26.7 %copy.114 = bf16[1,1,16,1024,576]{4,3,2,1,0:T(8,128)(2,1)} copy(bf16[1,1,16,1024,576]{3,4,2,1,0:T(8,128)(2,1)} %param.10) | data formatting | bytes 37748736 | tf_op args[3]
  41.2 1.7 %fusion.46 = (f32[4,64]{1,0:T(4,128)S(1)}, f32[4,64,256]{2,1,0:T(8,128)S(1)}) fusion(bf16[4,64,576]{2,1,0:T(8,128)(2,1)S(1)} %copy-done.2, bf16[4,256,576]{1,2,0:T(8,128)(2,1)} %param.8, pred[4,256]{1,0:T(4,128)(4,1)S(1)} %iota_compare_fusion.1), kind=kOutput, calls=%fused_computation.66 | convolution fusion | flops 75693824 | bytes 1738752 | tf_op jit(solution)/shard_map/phd,ptd->pht/dot_general | solution.py:30
  43.0 8.4 %fusion.4 = (f32[16,64]{1,0:T(8,128)S(1)}, f32[16,64,1024]{2,1,0:T(8,128)S(1)}) fusion(pred[16,1024]{1,0:T(8,128)(4,1)S(1)} %iota_compare_fusion, bf16[16,64,576]{2,1,0:T(8,128)(2,1)S(1)} %all-to-all-done, bf16[1,1,16,1024,576]{3,4,2,1,0:T(8,128)(2,1)} %param.10), kind=kOutput, calls=%fused_computation.7 | convolution fusion | flops 1211104256 | bytes 24268800 | tf_op jit(solution)/shard_map/phd,ptd->pht/dot_general | solution.py:30
  51.3 2.0 %copy-done.1 = f32[16,64,1024]{2,1,0:T(8,128)} copy-done((f32[16,64,1024]{2,1,0:T(8,128)}, f32[16,64,1024]{2,1,0:T(8,128)S(1)}, u32[]{:S(2)}) %copy-start.1) | copy-done | bytes 4194328
  53.3 1.2 fusion.6
  54.5 0.6 log_add_fusion
  55.1 6.7 %all-to-all-start.1 = ((f32[16,1,64]{2,1,0:T(1,128)}), f32[16,1,64]{2,1,0:T(1,128)S(1)}, u32[]{:S(2)}, u32[]{:S(2)}) async-start(f32[16,1,64]{2,1,0:T(1,128)} %bitcast.5), calls=%async_computation.1 | async-start | bytes 16384 | tf_op jit(solution)/shard_map/all_to_all | solution.py:75
  61.7 11.1 %broadcast_divide_fusion = bf16[16,64,512]{2,1,0:T(8,128)(2,1)} fusion(f32[16,64]{1,0:T(8,128)S(1)} %fusion.6, bf16[16,1024,576]{2,1,0:T(8,128)(2,1)} %bitcast.48, f32[16,64,1024]{2,1,0:T(8,128)} %copy-done.1, f32[16,64]{1,0:T(8,128)S(1)} %get-tuple-element.9, pred[16,1024]{1,0:T(8,128)(4,1)S(1)} %iota_compare_fusion), kind=kOutput, calls=%fused_computation.25 | convolution fusion | flops 1078984704 | bytes 22044672 | tf_op jit(solution)/shard_map/pht,ptd->phd/dot_general | solution.py:39
  72.9 6.8 %all-to-all-start.2 = ((bf16[16,64,512]{2,1,0:T(8,128)(2,1)}), bf16[16,64,512]{2,1,0:T(8,128)(2,1)S(1)}, u32[]{:S(2)}, u32[]{:S(2)}) async-start(bf16[16,64,512]{2,1,0:T(8,128)(2,1)} %broadcast_divide_fusion), calls=%async_computation.2 | async-start | bytes 2097152 | tf_op jit(solution)/shard_map/all_to_all | solution.py:74
  79.9 0.7 copy.116
  80.6 1.5 %select_reduce_fusion = f32[4,64]{0,1:T(8,128)} fusion(f32[16,64]{0,1:T(8,128)} %copy.116, pred[16,4]{0,1:T(4,128)(4,1)} %iota_compare_fusion.2), kind=kLoop, calls=%fused_computation.35 | loop fusion | flops 7936 | bytes 5184 | tf_op jit(solution)/shard_map/reduce_max | solution.py:78
  82.1 0.8 copy.117
  82.9 0.7 copy.119
  83.6 1.6 %fusion.29 = f32[4,64]{0,1:T(8,128)} fusion(f32[4,64]{0,1:T(8,128)} %copy.119, f32[16,64]{0,1:T(8,128)} %copy.116, pred[16,4]{0,1:T(4,128)(4,1)} %iota_compare_fusion.2), kind=kLoop, calls=%fused_computation.37 | loop fusion | flops 12032 | bytes 6208 | tf_op jit(solution)/shard_map/reduce_sum | solution.py:82
  85.2 0.8 copy.122
  86.7 1.4 %copy.125 = f32[1,4,64,1]{3,2,1,0:T(8,128)} copy(f32[1,4,64,1]{2,1,3,0:T(4,128)} %fusion.39) | data formatting | bytes 2048 | tf_op jit(solution)/shard_map/add | solution.py:84
  88.7 6.0 %all-to-all-done.2 = bf16[16,64,512]{2,1,0:T(8,128)(2,1)S(1)} async-done(((bf16[16,64,512]{2,1,0:T(8,128)(2,1)}), bf16[16,64,512]{2,1,0:T(8,128)(2,1)S(1)}, u32[]{:S(2)}, u32[]{:S(2)}) %all-to-all-start.2) | async-done | bytes 1048608 | tf_op jit(solution)/shard_map/all_to_all | solution.py:74
  94.7 1.6 %fusion.8 = f32[64,512,4]{1,2,0:T(4,128)S(1)} fusion(bf16[16,64,512]{2,1,0:T(8,128)(2,1)S(1)} %all-to-all-done.2, f32[4,64]{0,1:T(8,128)} %copy.119, f32[16,64]{0,1:T(8,128)} %copy.116, pred[16,4]{0,1:T(4,128)(4,1)} %iota_compare_fusion.2), kind=kOutput, calls=%fused_computation.10 | convolution fusion | flops 4202496 | bytes 1578048 | tf_op jit(solution)/shard_map/pch,phd->chd/dot_general | solution.py:81
  96.2 1.2 %fusion.17 = f32[1,4,64,512]{3,2,1,0:T(8,128)S(1)} fusion(bf16[4,256,576]{1,2,0:T(8,128)(2,1)S(1)} %copy-done.3, f32[64,512,4]{1,2,0:T(4,128)S(1)} %fusion.8, f32[4,64]{1,0:T(4,128)} %get-tuple-element.7, f32[4,64]{1,0:T(4,128)S(1)} %fusion.27, f32[4,64]{1,0:T(4,128)} %get-tuple-element.8, f32[4,64,256]{2,1,0:T(8,128)S(1)} %get-tuple-element.12, ...), kind=kOutput, calls=%fused_computation.20 | convolution fusion | flops 67764224 | bytes 2365440 | tf_op jit(solution)/shard_map/pht,ptd->phd/dot_general | solution.py:39
  97.9 18.1 %all_to_all.34 = f32[1,4,64,513]{3,1,0,2:T(4,128)S(1)} all-to-all(f32[1,4,64,513]{3,1,0,2:T(4,128)S(1)} %copy.126), channel_id=1, replica_groups=mesh['dp'=16,'sub'=8] {'sub'}, dimensions={2} | all-to-all | bytes 1050624 | tf_op jit(solution)/shard_map/all_to_all | solution.py:17
  (34 shorter events, 4.1 us)
Async XLA Ops:
  0.0 116.6 %copy-start = (bf16[8,512,128]{2,1,0:T(8,128)(2,1)S(1)}, bf16[8,512,128]{2,1,0:T(8,128)(2,1)}, u32[]{:S(2)}) copy-start(bf16[8,512,128]{2,1,0:T(8,128)(2,1)} %param.13) | copy-start | bytes 3145732
  5.2 37.8 %all-to-all-start = ((bf16[16,64,576]{2,1,0:T(8,128)(2,1)}), bf16[16,64,576]{2,1,0:T(8,128)(2,1)S(1)}, u32[]{:S(2)}, u32[]{:S(2)}) async-start(bf16[16,64,576]{2,1,0:T(8,128)(2,1)} %reshape.179), calls=%async_computation | async-start | bytes 2621440 | tf_op jit(solution)/shard_map/all_to_all | solution.py:70
  13.8 26.7 %copy-start.5 = (s32[1,1,16]{2,1,0:T(1,128)S(1)}, s32[1,1,16]{2,1,0:T(1,128)}, u32[]{:S(2)}) copy-start(s32[1,1,16]{2,1,0:T(1,128)} %param.12) | copy-start | bytes 196
  13.8 27.3 %copy-start.7 = (s32[4,1]{0,1:T(1,128)S(1)}, s32[4,1]{0,1:T(1,128)}, u32[]{:S(2)}) copy-start(s32[4,1]{0,1:T(1,128)} %param.9) | copy-start | bytes 52
  13.8 27.4 %copy-start.6 = (s32[1,1,16]{2,1,0:T(1,128)S(1)}, s32[1,1,16]{2,1,0:T(1,128)}, u32[]{:S(2)}) copy-start(s32[1,1,16]{2,1,0:T(1,128)} %param.11) | copy-start | bytes 196
  13.8 27.4 %copy-start.2 = (bf16[4,64,576]{2,1,0:T(8,128)(2,1)S(1)}, bf16[4,64,576]{2,1,0:T(8,128)(2,1)}, u32[]{:S(2)}) copy-start(bf16[4,64,576]{2,1,0:T(8,128)(2,1)} %param.7) | copy-start | bytes 884740
  51.3 2.0 %copy-start.1 = (f32[16,64,1024]{2,1,0:T(8,128)}, f32[16,64,1024]{2,1,0:T(8,128)S(1)}, u32[]{:S(2)}) copy-start(f32[16,64,1024]{2,1,0:T(8,128)S(1)} %get-tuple-element.10) | copy-start | bytes 12582916
  55.1 17.8 %all-to-all-start.1 = ((f32[16,1,64]{2,1,0:T(1,128)}), f32[16,1,64]{2,1,0:T(1,128)S(1)}, u32[]{:S(2)}, u32[]{:S(2)}) async-start(f32[16,1,64]{2,1,0:T(1,128)} %bitcast.5), calls=%async_computation.1 | async-start | bytes 16384 | tf_op jit(solution)/shard_map/all_to_all | solution.py:75
  72.9 23.4 %copy-start.3 = (bf16[4,256,576]{1,2,0:T(8,128)(2,1)S(1)}, bf16[4,256,576]{1,2,0:T(8,128)(2,1)}, u32[]{:S(2)}) copy-start(bf16[4,256,576]{1,2,0:T(8,128)(2,1)} %param.8) | copy-start | bytes 3538948
  72.9 21.8 %all-to-all-start.2 = ((bf16[16,64,512]{2,1,0:T(8,128)(2,1)}), bf16[16,64,512]{2,1,0:T(8,128)(2,1)S(1)}, u32[]{:S(2)}, u32[]{:S(2)}) async-start(bf16[16,64,512]{2,1,0:T(8,128)(2,1)} %broadcast_divide_fusion), calls=%async_computation.2 | async-start | bytes 2097152 | tf_op jit(solution)/shard_map/all_to_all | solution.py:74
  94.7 2.8 %copy-start.4 = (f32[1,4,64,1]{3,2,1,0:T(8,128)S(1)}, f32[1,4,64,1]{3,2,1,0:T(8,128)}, u32[]{:S(2)}) copy-start(f32[1,4,64,1]{3,2,1,0:T(8,128)} %copy.125) | copy-start | bytes 3076
where the time goes:
time: 119 us; the launch traced here: 117 us
  local copies, waits for them, and re-layouts  38.2 us (32%)
  matrix products  25.4 us (21%)
  starting transfers between devices  22 us (18%)
  blocking collectives  18.1 us (15%)
  other arithmetic  7.58 us (6%)
  waiting for transfers between devices  5.97 us (5%)
    unnamed x17, local copies, waits for them, and re-layouts  28.7 us
    all_to_all x1, blocking collectives, side_by_side(): lax.all_to_all(both, axis, split_axis=split_dim, concat_axis=concat_dim,...  18.1 us
    dot_general x2, matrix products, attend(): jnp.einsum('pht,ptd->phd', weights, slot_cache[:, :, :DL], preferred_elem...  12.3 us
    dot_general x2, matrix products, attend(): jnp.einsum('phd,ptd->pht', queries, slot_cache, preferred_element_type=jn...  10.1 us
    all_to_all x1, starting transfers between devices, local(): lax.all_to_all(outgoing, 'dp', split_axis=0, concat_axis=0, tiled=True)  8.59 us
    all_to_all x1, starting transfers between devices, local(): lax.all_to_all(helper_out, 'dp', split_axis=0, concat_axis=0, tiled=True)  6.79 us
    all_to_all x1, starting transfers between devices, local(): lax.all_to_all(helper_lse, 'dp', split_axis=0, concat_axis=0, tiled=True)  6.65 us
    all_to_all x1, waiting for transfers between devices, local(): lax.all_to_all(helper_out, 'dp', split_axis=0, concat_axis=0, tiled=True)  5.96 us
  transfers between devices with their start and end apart: 3, of which 1 were waited for; matrix products, arithmetic and copies ran while one was open for 42% of the time, Pallas kernels for 0%

commit v1 on v0

v1 whole, which is shorter than its diff:
```python
import jax
import jax.numpy as jnp
from jax import lax
from jax.experimental import pallas as pl
from jax.experimental.pallas import tpu as pltpu
from jax.sharding import PartitionSpec as P

MESH = pl.DeviceIdType.MESH
DL = 512
scale2 = 192 ** (-0.5) * 1.4426950408889634
masked_score = -1e30


def offset(k):
    b, kk = k // 4, k % 4
    i = (kk + jnp.minimum(b, 1)) % 4
    return (2 * b) % 4 + b // 2, (2 * i) % 4 + i // 2


def attend(query, keys, length):
    scores = jnp.dot(query, keys, preferred_element_type=jnp.float32)
    position = lax.broadcasted_iota(jnp.int32, scores.shape, 1)
    scores = jnp.where(position < length, scores, masked_score)
    largest = jnp.max(scores, axis=1, keepdims=True)
    exponent = jnp.exp2((scores - largest) * scale2)
    total = jnp.sum(exponent, axis=1, keepdims=True)
    weighted = lax.dot_general(
        exponent.astype(jnp.bfloat16),
        keys[:DL],
        (((1,), (1,)), ((), ())),
        preferred_element_type=jnp.float32,
    )
    return weighted / total, largest * scale2 + jnp.log2(total)


def kernel(
    own_len,
    host_len,
    plan_s,
    plan_v,
    queries,
    own_hbm,
    host_hbm,
    value_up,
    out,
    own,
    cache,
    packed,
    q_out,
    q_in,
    plan_in,
    o_out,
    o_in,
    stat,
    s_out,
    s_in,
    latent,
    c_out,
    c_in,
    own_sem,
    cache_sem,
    qs_sem,
    qr_sem,
    ps_sem,
    pr_sem,
    os_sem,
    or_sem,
    ss_sem,
    sr_sem,
    cs_sem,
    cr_sem,
):
    dp, sub = lax.axis_index("dp"), lax.axis_index("sub")
    y, z = dp // 4, dp % 4

    def ahead(k):
        dy, dz = offset(k)
        return ((y + dy) % 4) * 4 + (z + dz) % 4

    def behind(k):
        dy, dz = offset(k)
        return ((y + 4 - dy) % 4) * 4 + (z + 4 - dz) % 4

    def cache_copy(k):
        return pltpu.make_async_copy(host_hbm.at[behind(k)], cache.at[k], cache_sem.at[k])

    def remote(source, target, send, receive, device):
        return pltpu.make_async_remote_copy(
            source, target, send, receive, device_id=device, device_id_type=MESH
        )

    own_copy = pltpu.make_async_copy(own_hbm, own, own_sem)
    own_copy.start()

    barrier = pltpu.get_barrier_semaphore()

    def greet_dp(k, carry):
        pl.semaphore_signal(barrier, inc=1, device_id=(ahead(k), sub), device_id_type=MESH)
        return carry

    def greet_sub(j, carry):
        pl.semaphore_signal(barrier, inc=1, device_id=(dp, (sub + j) % 8), device_id_type=MESH)
        return carry

    lax.fori_loop(1, 16, greet_dp, 0)
    lax.fori_loop(1, 8, greet_sub, 0)

    def fetch(k, carry):
        cache_copy(k).start()
        return carry

    lax.fori_loop(0, 16, fetch, 0)

    for r in range(4):
        for c in range(4):
            packed[r, 64 * c : 64 * c + 64, :] = queries[r, :, 128 * c : 128 * c + 128]
        packed[r, 256:288, :] = jnp.concatenate(
            [queries[r, :32, 512:576], queries[r, 32:, 512:576]], axis=1
        )

    q_in[0] = packed[plan_s[dp]]

    def select(k, carry):
        q_out[k] = packed[plan_s[ahead(k)]]
        return carry

    lax.fori_loop(1, 16, select, 0)

    lane = lax.broadcasted_iota(jnp.int32, (64, 128), 1)

    own_copy.wait()
    stat[...] = jnp.full((64, 128), masked_score, jnp.float32)

    def own_step(r, carry):
        weighted, lse = attend(queries[r], own[r], own_len[r])
        o_out[r] = weighted.astype(jnp.bfloat16).reshape(8, 8, DL)
        stat[...] = jnp.where(lane == 5 * r, lse, stat[...])
        return carry

    lax.fori_loop(0, 4, own_step, 0)

    pl.semaphore_wait(barrier, 22)

    def plan_copy(k):
        return remote(plan_v, plan_in.at[k], ps_sem.at[k], pr_sem.at[k], (ahead(k), sub))

    def query_copy(k):
        return remote(q_out.at[k], q_in.at[k], qs_sem.at[k], qr_sem.at[k], (ahead(k), sub))

    def send_query(k, carry):
        query_copy(k).start()
        plan_copy(k).start()
        return carry

    lax.fori_loop(1, 16, send_query, 0)
    plan_in[0] = plan_v[...]

    def send_unit(u):
        def one(j, carry):
            to = (sub + j) % 8
            remote(
                o_out.at[u, to], o_in.at[u, j - 1], os_sem.at[u], or_sem.at[u], (dp, to)
            ).start()
            return carry

        lax.fori_loop(1, 8, one, 0)

    def send_stat(b):
        s_out[b] = stat[...].reshape(8, 8, 128)

        def one(j, carry):
            to = (sub + j) % 8
            remote(
                s_out.at[b, to], s_in.at[b, j - 1], ss_sem.at[b], sr_sem.at[b], (dp, to)
            ).start()
            return carry

        lax.fori_loop(1, 8, one, 0)

    def send_own(u, carry):
        send_unit(u)
        return carry

    lax.fori_loop(0, 4, send_own, 0)
    send_stat(0)

    def step(k, kk):
        cache_copy(k).wait()

        @pl.when(k > 0)
        def _():
            query_copy(k).wait_recv()
            plan_copy(k).wait_recv()

        block = q_in[k]
        query = jnp.concatenate(
            [block[64 * c : 64 * c + 64] for c in range(4)]
            + [jnp.concatenate([block[256:288, :64], block[256:288, 64:]], axis=0)],
            axis=1,
        )
        weighted, lse = attend(query, cache[k], host_len[behind(k)])
        o_out[k + 4] = weighted.astype(jnp.bfloat16).reshape(8, 8, DL)
        lanes = lax.broadcasted_iota(jnp.int32, (1, 16), 1)
        request = jnp.sum(jnp.where(lanes == dp, plan_in[k], 0), axis=1, keepdims=True)
        stat[...] = jnp.where(lane == 4 * kk + request, lse, stat[...])
        send_unit(k + 4)

    def c_copy(k):
        return remote(c_out.at[k + 4], c_in.at[k], cs_sem.at[k], cr_sem.at[k], (behind(k), sub))

    def combine(b):
        def all_in(buffer, target, semaphore):
            return pltpu.make_async_copy(buffer.at[pl.ds(0, 7)], target, semaphore)

        all_in(s_out.at[b], s_in.at[b], sr_sem.at[b]).wait()
        for kk in range(4):
            u = 4 * b + kk
            all_in(o_out.at[u], o_in.at[u], or_sem.at[u]).wait()
        logs = [s_out[b, sub]] + [s_in[b, j] for j in range(7)]
        peak = logs[0]
        for value in logs[1:]:
            peak = jnp.maximum(peak, value)
        weights = [jnp.exp2(value - peak) for value in logs]
        total = weights[0]
        for value in weights[1:]:
            total = total + value
        lse = peak + jnp.log2(total)
        weights = [value / total for value in weights]
        for kk in range(4):
            u = 4 * b + kk
            sums = [jnp.zeros((8, DL), jnp.float32) for _ in range(4)]
            for j in range(8):
                piece = (o_out[u, sub] if j == 0 else o_in[u, j - 1]).astype(jnp.float32)
                for r in range(4):
                    at = 4 * kk + r
                    sums[r] = sums[r] + weights[j][:, at : at + 1] * piece
            for r in range(4):
                latent[4 * kk + r] = sums[r]
            c_out[u, 4] = lse if kk == 0 else pltpu.roll(lse, 128 - 4 * kk, 1)
        for h in range(8):
            rows = latent[:, h, :].astype(jnp.bfloat16)
            value = jnp.dot(rows, value_up[h], preferred_element_type=jnp.float32)
            for kk in range(4):
                c_out[4 * b + kk, 0:4, h, :] = value[4 * kk : 4 * kk + 4]

    def batch(b, carry):
        @pl.when(b < 4)
        def _():
            stat[...] = jnp.full((64, 128), masked_score, jnp.float32)

            def pair(i, carry):
                for t in range(2):
                    step(4 * b + 2 * i + t, 2 * i + t)
                return carry

            lax.fori_loop(0, 2, pair, 0)
            send_stat(b + 1)

        combine(b)

        @pl.when(b > 0)
        def _():
            def send(kk, carry):
                k = 4 * b - 4 + kk

                @pl.when(k > 0)
                def _():
                    c_copy(k).start()

                return carry

            lax.fori_loop(0, 4, send, 0)

        return carry

    lax.fori_loop(0, 5, batch, 0)

    def arrive(k, carry):
        c_copy(k).wait_recv()
        return carry

    lax.fori_loop(1, 16, arrive, 0)

    def contribution(u):
        return c_out.at[u] if u < 5 else c_in.at[u - 4]

    peak = contribution(0)[4]
    for u in range(1, 20):
        peak = jnp.maximum(peak, contribution(u)[4])
    total = jnp.zeros((8, 128), jnp.float32)
    sums = [jnp.zeros((8, 128), jnp.float32) for _ in range(4)]
    for u in range(20):
        weight = jnp.exp2(contribution(u)[4] - peak)
        total = total + weight
        for r in range(4):
            sums[r] = sums[r] + weight[:, r : r + 1] * contribution(u)[r]
    for r in range(4):
        out[r] = (sums[r] / total[:, r : r + 1]).astype(out.dtype)

    def finish(k, carry):
        query_copy(k).wait_send()
        plan_copy(k).wait_send()
        c_copy(k).wait_send()
        return carry

    lax.fori_loop(1, 16, finish, 0)

    def sent(u, carry):
        pltpu.make_async_copy(o_out.at[u, pl.ds(0, 7)], o_in.at[u], os_sem.at[u]).wait()
        return carry

    lax.fori_loop(0, 20, sent, 0)

    def sent_stat(b, carry):
        pltpu.make_async_copy(s_out.at[b, pl.ds(0, 7)], s_in.at[b], ss_sem.at[b]).wait()
        return carry

    lax.fori_loop(0, 5, sent_stat, 0)


def local(queries, own_cache, own_len, host_cache, host_len, page_plan, value_up):
    bf16, f32 = jnp.bfloat16, jnp.float32
    host = jnp.swapaxes(host_cache, 3, 4).reshape(16, 576, 1024)
    own = jnp.swapaxes(own_cache, 1, 2)
    vmem = pl.BlockSpec(memory_space=pltpu.VMEM)
    smem = pl.BlockSpec(memory_space=pltpu.SMEM)
    anywhere = pl.BlockSpec(memory_space=pl.ANY)
    dma = pltpu.SemaphoreType.DMA
    return pl.pallas_call(
        kernel,
        out_shape=jax.ShapeDtypeStruct((4, 8, 128), bf16),
        in_specs=[smem, smem, smem, vmem, vmem, anywhere, anywhere, vmem],
        out_specs=vmem,
        scratch_shapes=[
            pltpu.VMEM((4, 576, 256), bf16),
            pltpu.VMEM((16, 576, 1024), bf16),
            pltpu.VMEM((4, 288, 128), bf16),
            pltpu.VMEM((16, 288, 128), bf16),
            pltpu.VMEM((16, 288, 128), bf16),
            pltpu.VMEM((16, 1, 16), jnp.int32),
            pltpu.VMEM((20, 8, 8, DL), bf16),
            pltpu.VMEM((20, 7, 8, DL), bf16),
            pltpu.VMEM((64, 128), f32),
            pltpu.VMEM((5, 8, 8, 128), f32),
            pltpu.VMEM((5, 7, 8, 128), f32),
            pltpu.VMEM((16, 8, DL), f32),
            pltpu.VMEM((20, 5, 8, 128), f32),
            pltpu.VMEM((16, 5, 8, 128), f32),
            dma,
            dma((16,)),
            dma((16,)),
            dma((16,)),
            dma((16,)),
            dma((16,)),
            dma((20,)),
            dma((20,)),
            dma((5,)),
            dma((5,)),
            dma((16,)),
            dma((16,)),
        ],
        compiler_params=pltpu.CompilerParams(
            vmem_limit_bytes=60 * 2**20, collective_id=0, has_side_effects=True
        ),
    )(
        own_len.reshape(4),
        host_len.reshape(16),
        page_plan.reshape(16),
        page_plan.reshape(1, 16),
        queries,
        own,
        host,
        value_up,
    )


def solution(mesh):
    return jax.shard_map(
        local,
        mesh=mesh,
        in_specs=(
            P("dp", None, None),
            P("dp", "sub", None),
            P("dp", "sub"),
            P("dp", "sub", None, None, None),
            P("dp", "sub", None),
            P("dp", "sub", None),
            P("sub", None, None),
        ),
        out_specs=P("dp", "sub", None),
        check_vma=False,
    )
```

time: 119 us -> 55.1 us (0.46); the launches traced: 117 us -> 54.9 us
  Pallas kernels: 0 us -> 53.6 us
  local copies, waits for them, and re-layouts: 38.2 us -> 1.3 us
  matrix products: 25.4 us -> 0 us
  starting transfers between devices: 22 us -> 0 us
  blocking collectives: 18.1 us -> 0 us
  other arithmetic: 7.58 us -> 0 us
  waiting for transfers between devices: 5.97 us -> 0 us
    pallas_call x0 -> x1, Pallas kernels: none -> 53.6 us  [local(): pl.pallas_call(kernel, out_shape=jax.ShapeDtypeStruct((4, 8, 128), bf16),...]
    unnamed x17 -> x1, local copies, waits for them, and re-layouts: 28.7 us -> 1.3 us
    dot_general x7 -> x0, matrix products: 25.4 us -> none  [the longest x2 12.3 us: attend(): jnp.einsum('pht,ptd->phd', weights, slot_cache[:, :, :DL], preferred_elem...]
    all_to_all x3 -> x0, starting transfers between devices: 22 us -> none  [the longest x1 8.59 us: local(): lax.all_to_all(outgoing, 'dp', split_axis=0, concat_axis=0, tiled=True)]
    all_to_all x1 -> x0, blocking collectives: 18.1 us -> none  [side_by_side(): lax.all_to_all(both, axis, split_axis=split_dim, concat_axis=concat_dim,...]
    all_to_all x3 -> x0, waiting for transfers between devices: 5.97 us -> none  [the longest x1 5.96 us: local(): lax.all_to_all(helper_out, 'dp', split_axis=0, concat_axis=0, tiled=True)]
    reshape x2 -> x0, local copies, waits for them, and re-layouts: 3.95 us -> none  [the longest x1 2.49 us: local(): outgoing = outgoing.astype(jnp.bfloat16).reshape(groups, head_count, width)]
    reduce_sum x5 -> x0, other arithmetic: 3.07 us -> none  [the longest x1 1.6 us: local(): totals = own_weight + jnp.sum(help_weight, axis=0)]
  transfers between devices with their start and end apart: 3 -> 0, of which waited for: 1 -> 0; matrix products, arithmetic and copies ran while one was open for 42% -> 0% of each run, Pallas kernels for 0% -> 0%
where the time goes in v1:
time: 55.1 us; the launch traced here: 54.9 us
  Pallas kernels  53.6 us (97%)
  local copies, waits for them, and re-layouts  1.3 us (2%)
    pallas_call x1, Pallas kernels, local(): pl.pallas_call(kernel, out_shape=jax.ShapeDtypeStruct((4, 8, 128), bf16),...  53.6 us
    unnamed x1, local copies, waits for them, and re-layouts  1.3 us

profile of v1, /device:TPU:1, one launch (start us, length us, event | category | flops | bytes accessed | tf_op | source)
XLA Modules:
  0.0 54.9 jit_solution(981682893166926215)
XLA Ops:
  0.0 53.6 %shard_map.73 = bf16[4,8,128]{2,1,0:T(8,128)(2,1)} custom-call(s32[4]{0:T(128)} %bitcast.12, s32[16]{0:T(128)} %bitcast.13, s32[16]{0:T(128)} %bitcast.10, s32[1,16]{1,0:T(1,128)} %bitcast.11, bf16[4,64,576]{2,1,0:T(8,128)(2,1)} %queries.1, bf16[4,576,256]{2,1,0:T(8,128)(2,1)} %bitcast.9, bf16[16,576,1024]{2,1,0:T(8,128)(2,1)} %bitcast.8, ...), custom_call_target="tpu_custom_call" | custom-call | tf_op jit(solution)/shard_map/pallas_call | solution.py:329
  53.6 1.3 %copy.9 = bf16[4,8,128]{2,1,0:T(8,128)(2,1)} copy(bf16[4,8,128]{2,1,0:T(8,128)(2,1)} %shard_map.73) | data formatting | bytes 16384

commit v2 on v1

--- a/solution.py
+++ b/solution.py
@@ -11,14 +11,23 @@
 masked_score = -1e30
 
 
+STEPS = [(0, 0), (2, 2), (2, 3), (3, 2), (2, 1), (1, 2), (2, 0), (0, 2)]
+STEPS += [(3, 1), (1, 3), (3, 3), (1, 1), (3, 0), (0, 3), (1, 0), (0, 1)]
+
+
 def offset(k):
-    b, kk = k // 4, k % 4
-    i = (kk + jnp.minimum(b, 1)) % 4
-    return (2 * b) % 4 + b // 2, (2 * i) % 4 + i // 2
-
-
-def attend(query, keys, length):
-    scores = jnp.dot(query, keys, preferred_element_type=jnp.float32)
+    if isinstance(k, int):
+        return STEPS[k]
+    words = [sum(step[i] << (2 * n) for n, step in enumerate(STEPS)) for i in range(2)]
+    words = [jnp.int32(word - (1 << 32) if word >= 1 << 31 else word) for word in words]
+    return tuple(lax.shift_right_logical(word, 2 * k) & 3 for word in words)
+
+
+def score(query, keys):
+    return jnp.dot(query, keys, preferred_element_type=jnp.float32)
+
+
+def attend(scores, keys, length):
     position = lax.broadcasted_iota(jnp.int32, scores.shape, 1)
     scores = jnp.where(position < length, scores, masked_score)
     largest = jnp.max(scores, axis=1, keepdims=True)
@@ -38,11 +47,13 @@
     host_len,
     plan_s,
     plan_v,
-    queries,
+    queries_hbm,
     own_hbm,
     host_hbm,
+    value_hbm,
+    out,
+    queries,
     value_up,
-    out,
     own,
     cache,
     packed,
@@ -54,9 +65,12 @@
     stat,
     s_out,
     s_in,
+    score_buffer,
     latent,
     c_out,
     c_in,
+    query_sem,
+    value_sem,
     own_sem,
     cache_sem,
     qs_sem,
@@ -75,11 +89,14 @@
 
     def ahead(k):
         dy, dz = offset(k)
-        return ((y + dy) % 4) * 4 + (z + dz) % 4
+        return ((y + dy) & 3) * 4 + ((z + dz) & 3)
 
     def behind(k):
         dy, dz = offset(k)
-        return ((y + 4 - dy) % 4) * 4 + (z + 4 - dz) % 4
+        return ((y + 4 - dy) & 3) * 4 + ((z + 4 - dz) & 3)
+
+    def peer(j):
+        return (sub + j) & 7
 
     def cache_copy(k):
         return pltpu.make_async_copy(host_hbm.at[behind(k)], cache.at[k], cache_sem.at[k])
@@ -89,28 +106,25 @@
             source, target, send, receive, device_id=device, device_id_type=MESH
         )
 
+    query_fetch = pltpu.make_async_copy(queries_hbm, queries, query_sem)
+    query_fetch.start()
     own_copy = pltpu.make_async_copy(own_hbm, own, own_sem)
     own_copy.start()
-
     barrier = pltpu.get_barrier_semaphore()
-
-    def greet_dp(k, carry):
+    for k in range(1, 16):
         pl.semaphore_signal(barrier, inc=1, device_id=(ahead(k), sub), device_id_type=MESH)
-        return carry
-
-    def greet_sub(j, carry):
-        pl.semaphore_signal(barrier, inc=1, device_id=(dp, (sub + j) % 8), device_id_type=MESH)
-        return carry
-
-    lax.fori_loop(1, 16, greet_dp, 0)
-    lax.fori_loop(1, 8, greet_sub, 0)
+    for j in range(1, 8):
+        pl.semaphore_signal(barrier, inc=1, device_id=(dp, peer(j)), device_id_type=MESH)
 
     def fetch(k, carry):
         cache_copy(k).start()
         return carry
 
     lax.fori_loop(0, 16, fetch, 0)
-
+    value_copy = pltpu.make_async_copy(value_hbm, value_up, value_sem)
+    value_copy.start()
+
+    query_fetch.wait()
     for r in range(4):
         for c in range(4):
             packed[r, 64 * c : 64 * c + 64, :] = queries[r, :, 128 * c : 128 * c + 128]
@@ -118,73 +132,66 @@
             [queries[r, :32, 512:576], queries[r, 32:, 512:576]], axis=1
         )
 
-    q_in[0] = packed[plan_s[dp]]
-
     def select(k, carry):
         q_out[k] = packed[plan_s[ahead(k)]]
         return carry
 
     lax.fori_loop(1, 16, select, 0)
 
-    lane = lax.broadcasted_iota(jnp.int32, (64, 128), 1)
-
-    own_copy.wait()
-    stat[...] = jnp.full((64, 128), masked_score, jnp.float32)
-
-    def own_step(r, carry):
-        weighted, lse = attend(queries[r], own[r], own_len[r])
-        o_out[r] = weighted.astype(jnp.bfloat16).reshape(8, 8, DL)
-        stat[...] = jnp.where(lane == 5 * r, lse, stat[...])
-        return carry
-
-    lax.fori_loop(0, 4, own_step, 0)
-
-    pl.semaphore_wait(barrier, 22)
-
     def plan_copy(k):
         return remote(plan_v, plan_in.at[k], ps_sem.at[k], pr_sem.at[k], (ahead(k), sub))
 
     def query_copy(k):
         return remote(q_out.at[k], q_in.at[k], qs_sem.at[k], qr_sem.at[k], (ahead(k), sub))
 
+    pl.semaphore_wait(barrier, 22)
+
     def send_query(k, carry):
         query_copy(k).start()
+        return carry
+
+    def send_plan(k, carry):
         plan_copy(k).start()
         return carry
 
+    lax.fori_loop(1, 16, send_plan, 0)
     lax.fori_loop(1, 16, send_query, 0)
+
+    q_in[0] = packed[plan_s[dp]]
     plan_in[0] = plan_v[...]
 
     def send_unit(u):
-        def one(j, carry):
-            to = (sub + j) % 8
+        for j in range(1, 8):
+            to = peer(j)
             remote(
                 o_out.at[u, to], o_in.at[u, j - 1], os_sem.at[u], or_sem.at[u], (dp, to)
             ).start()
-            return carry
-
-        lax.fori_loop(1, 8, one, 0)
 
     def send_stat(b):
         s_out[b] = stat[...].reshape(8, 8, 128)
-
-        def one(j, carry):
-            to = (sub + j) % 8
+        for j in range(1, 8):
+            to = peer(j)
             remote(
                 s_out.at[b, to], s_in.at[b, j - 1], ss_sem.at[b], sr_sem.at[b], (dp, to)
             ).start()
-            return carry
-
-        lax.fori_loop(1, 8, one, 0)
-
-    def send_own(u, carry):
-        send_unit(u)
-        return carry
-
-    lax.fori_loop(0, 4, send_own, 0)
+        stat[...] = jnp.full((64, 128), masked_score, jnp.float32)
+
+    lane = lax.broadcasted_iota(jnp.int32, (64, 128), 1)
+
+    own_copy.wait()
+    stat[...] = jnp.full((64, 128), masked_score, jnp.float32)
+
+    def own_step(r, carry):
+        weighted, lse = attend(score(queries[r], own[r]), own[r], own_len[r])
+        o_out[r] = weighted.astype(jnp.bfloat16).reshape(8, 8, DL)
+        stat[...] = jnp.where(lane == 5 * r, lse, stat[...])
+        send_unit(r)
+        return carry
+
+    lax.fori_loop(0, 4, own_step, 0)
     send_stat(0)
 
-    def step(k, kk):
+    def prepare(k):
         cache_copy(k).wait()
 
         @pl.when(k > 0)
@@ -192,17 +199,27 @@
             query_copy(k).wait_recv()
             plan_copy(k).wait_recv()
 
+    def score_step(k):
         block = q_in[k]
         query = jnp.concatenate(
             [block[64 * c : 64 * c + 64] for c in range(4)]
             + [jnp.concatenate([block[256:288, :64], block[256:288, 64:]], axis=0)],
             axis=1,
         )
-        weighted, lse = attend(query, cache[k], host_len[behind(k)])
+        return score(query, cache[k])
+
+    def step(k, t, last):
+        if not last:
+            prepare(k + 1)
+            scores = score_buffer[t]
+            score_buffer[1 - t] = score_step(k + 1)
+        else:
+            scores = score_buffer[t]
+        weighted, lse = attend(scores, cache[k], host_len[behind(k)])
         o_out[k + 4] = weighted.astype(jnp.bfloat16).reshape(8, 8, DL)
         lanes = lax.broadcasted_iota(jnp.int32, (1, 16), 1)
         request = jnp.sum(jnp.where(lanes == dp, plan_in[k], 0), axis=1, keepdims=True)
-        stat[...] = jnp.where(lane == 4 * kk + request, lse, stat[...])
+        stat[...] = jnp.where(lane == 4 * (k % 4) + request, lse, stat[...])
         send_unit(k + 4)
 
     def c_copy(k):
@@ -243,37 +260,41 @@
             for kk in range(4):
                 c_out[4 * b + kk, 0:4, h, :] = value[4 * kk : 4 * kk + 4]
 
-    def batch(b, carry):
-        @pl.when(b < 4)
+    def send_back(b):
+        for kk in range(4):
+            k = 4 * b - 4 + kk
+
+            @pl.when(k > 0)
+            def _():
+                c_copy(k).start()
+
+    prepare(0)
+    score_buffer[0] = score_step(0)
+    value_copy.wait()
+
+    def pair(i, carry):
+        for t in range(2):
+            step(2 * i + t, t, False)
+
+        @pl.when(i % 2 == 1)
         def _():
-            stat[...] = jnp.full((64, 128), masked_score, jnp.float32)
-
-            def pair(i, carry):
-                for t in range(2):
-                    step(4 * b + 2 * i + t, 2 * i + t)
-                return carry
-
-            lax.fori_loop(0, 2, pair, 0)
-            send_stat(b + 1)
-
-        combine(b)
-
-        @pl.when(b > 0)
+            send_stat(i // 2 + 1)
+
+        @pl.when((i % 2 == 0) & (i > 0))
         def _():
-            def send(kk, carry):
-                k = 4 * b - 4 + kk
-
-                @pl.when(k > 0)
-                def _():
-                    c_copy(k).start()
-
-                return carry
-
-            lax.fori_loop(0, 4, send, 0)
-
-        return carry
-
-    lax.fori_loop(0, 5, batch, 0)
+            combine(i // 2 - 1)
+            send_back(i // 2 - 1)
+
+        return carry
+
+    lax.fori_loop(0, 7, pair, 0)
+    step(14, 0, False)
+    step(15, 1, True)
+    send_stat(4)
+    combine(3)
+    send_back(3)
+    combine(4)
+    send_back(4)
 
     def arrive(k, carry):
         c_copy(k).wait_recv()
@@ -329,9 +350,11 @@
     return pl.pallas_call(
         kernel,
         out_shape=jax.ShapeDtypeStruct((4, 8, 128), bf16),
-        in_specs=[smem, smem, smem, vmem, vmem, anywhere, anywhere, vmem],
+        in_specs=[smem, smem, smem, vmem, anywhere, anywhere, anywhere, anywhere],
         out_specs=vmem,
         scratch_shapes=[
+            pltpu.VMEM((4, 64, 576), bf16),
+            pltpu.VMEM((8, DL, 128), bf16),
             pltpu.VMEM((4, 576, 256), bf16),
             pltpu.VMEM((16, 576, 1024), bf16),
             pltpu.VMEM((4, 288, 128), bf16),
@@ -343,9 +366,12 @@
             pltpu.VMEM((64, 128), f32),
             pltpu.VMEM((5, 8, 8, 128), f32),
             pltpu.VMEM((5, 7, 8, 128), f32),
+            pltpu.VMEM((2, 64, 1024), f32),
             pltpu.VMEM((16, 8, DL), f32),
             pltpu.VMEM((20, 5, 8, 128), f32),
             pltpu.VMEM((16, 5, 8, 128), f32),
+            dma,
+            dma,
             dma,
             dma((16,)),
             dma((16,)),

time: 55.1 us -> 43.7 us (0.79)
  Pallas kernels: 53.6 us -> 42.2 us
    pallas_call x1, Pallas kernels: 53.6 us -> 42.2 us  [local(): pl.pallas_call(kernel, out_shape=jax.ShapeDtypeStruct((4, 8, 128), bf16),...]
where the time goes in v2:
time: 43.7 us; the launch traced here: 43.5 us
  Pallas kernels  42.2 us (97%)
  local copies, waits for them, and re-layouts  1.3 us (3%)
    pallas_call x1, Pallas kernels, local(): pl.pallas_call(kernel, out_shape=jax.ShapeDtypeStruct((4, 8, 128), bf16),...  42.2 us
    unnamed x1, local copies, waits for them, and re-layouts  1.3 us

profile of v2, /device:TPU:1, one launch (start us, length us, event | category | flops | bytes accessed | tf_op | source)
XLA Modules:
  0.0 43.5 jit_solution(9496213504297270678)
XLA Ops:
  0.0 42.2 %shard_map.73 = bf16[4,8,128]{2,1,0:T(8,128)(2,1)} custom-call(s32[4]{0:T(128)} %bitcast.12, s32[16]{0:T(128)} %bitcast.13, s32[16]{0:T(128)} %bitcast.10, s32[1,16]{1,0:T(1,128)} %bitcast.11, bf16[4,64,576]{2,1,0:T(8,128)(2,1)} %queries_hbm.1, bf16[4,576,256]{2,1,0:T(8,128)(2,1)} %bitcast.9, bf16[16,576,1024]{2,1,0:T(8,128)(2,1)} %bitcast.8, ...), custom_call_target="tpu_custom_call" | custom-call | tf_op jit(solution)/shard_map/pallas_call | solution.py:350
  42.2 1.3 %copy.9 = bf16[4,8,128]{2,1,0:T(8,128)(2,1)} copy(bf16[4,8,128]{2,1,0:T(8,128)(2,1)} %shard_map.73) | data formatting | bytes 16384

commit v3 on v2

--- a/solution.py
+++ b/solution.py
@@ -121,8 +121,20 @@
         return carry
 
     lax.fori_loop(0, 16, fetch, 0)
-    value_copy = pltpu.make_async_copy(value_hbm, value_up, value_sem)
-    value_copy.start()
+
+    def value_copy(h):
+        half = value_up.at[h // 2, :, 128 * (h % 2) : 128 * (h % 2) + 128]
+        return pltpu.make_async_copy(value_hbm.at[h], half, value_sem.at[h])
+
+    for h in range(8):
+        value_copy(h).start()
+
+    def value_wait():
+        for h in range(8):
+            value_copy(h).wait()
+
+    o_out[4] = jnp.zeros((8, 8, DL), jnp.bfloat16)
+    o_in[4] = jnp.zeros((7, 8, DL), jnp.bfloat16)
 
     query_fetch.wait()
     for r in range(4):
@@ -216,23 +228,27 @@
         else:
             scores = score_buffer[t]
         weighted, lse = attend(scores, cache[k], host_len[behind(k)])
-        o_out[k + 4] = weighted.astype(jnp.bfloat16).reshape(8, 8, DL)
+        o_out[k + 5] = weighted.astype(jnp.bfloat16).reshape(8, 8, DL)
         lanes = lax.broadcasted_iota(jnp.int32, (1, 16), 1)
         request = jnp.sum(jnp.where(lanes == dp, plan_in[k], 0), axis=1, keepdims=True)
-        stat[...] = jnp.where(lane == 4 * (k % 4) + request, lse, stat[...])
-        send_unit(k + 4)
+        stat[...] = jnp.where(lane == 4 * ((k + 1) % 4) + request, lse, stat[...])
+        send_unit(k + 5)
 
     def c_copy(k):
-        return remote(c_out.at[k + 4], c_in.at[k], cs_sem.at[k], cr_sem.at[k], (behind(k), sub))
-
-    def combine(b):
+        return remote(c_out.at[k + 5], c_in.at[k], cs_sem.at[k], cr_sem.at[k], (behind(k), sub))
+
+    def combine(b, count=4):
         def all_in(buffer, target, semaphore):
             return pltpu.make_async_copy(buffer.at[pl.ds(0, 7)], target, semaphore)
 
         all_in(s_out.at[b], s_in.at[b], sr_sem.at[b]).wait()
-        for kk in range(4):
+        for kk in range(count):
             u = 4 * b + kk
-            all_in(o_out.at[u], o_in.at[u], or_sem.at[u]).wait()
+
+            @pl.when(u != 4)
+            def _():
+                all_in(o_out.at[u], o_in.at[u], or_sem.at[u]).wait()
+
         logs = [s_out[b, sub]] + [s_in[b, j] for j in range(7)]
         peak = logs[0]
         for value in logs[1:]:
@@ -243,7 +259,7 @@
             total = total + value
         lse = peak + jnp.log2(total)
         weights = [value / total for value in weights]
-        for kk in range(4):
+        for kk in range(count):
             u = 4 * b + kk
             sums = [jnp.zeros((8, DL), jnp.float32) for _ in range(4)]
             for j in range(8):
@@ -254,89 +270,102 @@
             for r in range(4):
                 latent[4 * kk + r] = sums[r]
             c_out[u, 4] = lse if kk == 0 else pltpu.roll(lse, 128 - 4 * kk, 1)
-        for h in range(8):
-            rows = latent[:, h, :].astype(jnp.bfloat16)
-            value = jnp.dot(rows, value_up[h], preferred_element_type=jnp.float32)
-            for kk in range(4):
-                c_out[4 * b + kk, 0:4, h, :] = value[4 * kk : 4 * kk + 4]
-
-    def send_back(b):
-        for kk in range(4):
-            k = 4 * b - 4 + kk
+        rows = 4 * count
+        for h in range(0, 8, 2):
+            both = jnp.concatenate([latent[:rows, h, :], latent[:rows, h + 1, :]], axis=0)
+            value = jnp.dot(
+                both.astype(jnp.bfloat16), value_up[h // 2], preferred_element_type=jnp.float32
+            )
+            for kk in range(count):
+                at = 4 * kk
+                c_out[4 * b + kk, 0:4, h, :] = value[at : at + 4, :128]
+                c_out[4 * b + kk, 0:4, h + 1, :] = value[rows + at : rows + at + 4, 128:]
+
+    def send_back(b, count=4):
+        for kk in range(count):
+            k = 4 * b + kk - 5
 
             @pl.when(k > 0)
             def _():
                 c_copy(k).start()
 
-    prepare(0)
+    cache_copy(0).wait()
     score_buffer[0] = score_step(0)
-    value_copy.wait()
+    step(0, 0, True)
+    for k in (1, 2):
+        prepare(k)
+        score_buffer[0] = score_step(k)
+        step(k, 0, True)
+    send_stat(1)
+    value_wait()
+    combine(0)
+    prepare(3)
+    score_buffer[1] = score_step(3)
 
     def pair(i, carry):
-        for t in range(2):
-            step(2 * i + t, t, False)
-
-        @pl.when(i % 2 == 1)
+        step(2 * i + 1, 1, False)
+        step(2 * i + 2, 0, False)
+
+        @pl.when(i % 2 == 0)
         def _():
             send_stat(i // 2 + 1)
 
-        @pl.when((i % 2 == 0) & (i > 0))
-        def _():
-            combine(i // 2 - 1)
-            send_back(i // 2 - 1)
-
-        return carry
-
-    lax.fori_loop(0, 7, pair, 0)
-    step(14, 0, False)
+        return carry
+
+    lax.fori_loop(1, 7, pair, 0)
     step(15, 1, True)
-    send_stat(4)
-    combine(3)
-    send_back(3)
-    combine(4)
-    send_back(4)
-
-    def arrive(k, carry):
-        c_copy(k).wait_recv()
-        return carry
-
-    lax.fori_loop(1, 16, arrive, 0)
-
-    def contribution(u):
-        return c_out.at[u] if u < 5 else c_in.at[u - 4]
-
-    peak = contribution(0)[4]
-    for u in range(1, 20):
-        peak = jnp.maximum(peak, contribution(u)[4])
-    total = jnp.zeros((8, 128), jnp.float32)
-    sums = [jnp.zeros((8, 128), jnp.float32) for _ in range(4)]
-    for u in range(20):
-        weight = jnp.exp2(contribution(u)[4] - peak)
-        total = total + weight
-        for r in range(4):
-            sums[r] = sums[r] + weight[:, r : r + 1] * contribution(u)[r]
-    for r in range(4):
-        out[r] = (sums[r] / total[:, r : r + 1]).astype(out.dtype)
+    send_stat(5)
+
+    def late(b, carry):
+        combine(b)
+        send_back(b)
+        return carry
+
+    lax.fori_loop(1, 5, late, 0)
+    combine(5, 1)
+    send_back(5, 1)
 
     def finish(k, carry):
         query_copy(k).wait_send()
         plan_copy(k).wait_send()
-        c_copy(k).wait_send()
         return carry
 
     lax.fori_loop(1, 16, finish, 0)
 
     def sent(u, carry):
-        pltpu.make_async_copy(o_out.at[u, pl.ds(0, 7)], o_in.at[u], os_sem.at[u]).wait()
-        return carry
-
-    lax.fori_loop(0, 20, sent, 0)
+        @pl.when(u != 4)
+        def _():
+            pltpu.make_async_copy(o_out.at[u, pl.ds(0, 7)], o_in.at[u], os_sem.at[u]).wait()
+
+        return carry
+
+    lax.fori_loop(0, 21, sent, 0)
 
     def sent_stat(b, carry):
         pltpu.make_async_copy(s_out.at[b, pl.ds(0, 7)], s_in.at[b], ss_sem.at[b]).wait()
         return carry
 
-    lax.fori_loop(0, 5, sent_stat, 0)
+    lax.fori_loop(0, 6, sent_stat, 0)
+
+    def arrive(k, carry):
+        c_copy(k).wait()
+        return carry
+
+    lax.fori_loop(1, 16, arrive, 0)
+
+    parts = [c_out.at[u] for u in (0, 1, 2, 3, 5)] + [c_in.at[k] for k in range(1, 16)]
+    peak = parts[0][4]
+    for part in parts[1:]:
+        peak = jnp.maximum(peak, part[4])
+    total = jnp.zeros((8, 128), jnp.float32)
+    sums = [jnp.zeros((8, 128), jnp.float32) for _ in range(4)]
+    for part in parts:
+        weight = jnp.exp2(part[4] - peak)
+        total = total + weight
+        for r in range(4):
+            sums[r] = sums[r] + weight[:, r : r + 1] * part[r]
+    for r in range(4):
+        out[r] = (sums[r] / total[:, r : r + 1]).astype(out.dtype)
 
 
 def local(queries, own_cache, own_len, host_cache, host_len, page_plan, value_up):
@@ -354,34 +383,34 @@
         out_specs=vmem,
         scratch_shapes=[
             pltpu.VMEM((4, 64, 576), bf16),
-            pltpu.VMEM((8, DL, 128), bf16),
+            pltpu.VMEM((4, DL, 256), bf16),
             pltpu.VMEM((4, 576, 256), bf16),
             pltpu.VMEM((16, 576, 1024), bf16),
             pltpu.VMEM((4, 288, 128), bf16),
             pltpu.VMEM((16, 288, 128), bf16),
             pltpu.VMEM((16, 288, 128), bf16),
             pltpu.VMEM((16, 1, 16), jnp.int32),
-            pltpu.VMEM((20, 8, 8, DL), bf16),
-            pltpu.VMEM((20, 7, 8, DL), bf16),
+            pltpu.VMEM((21, 8, 8, DL), bf16),
+            pltpu.VMEM((21, 7, 8, DL), bf16),
             pltpu.VMEM((64, 128), f32),
-            pltpu.VMEM((5, 8, 8, 128), f32),
-            pltpu.VMEM((5, 7, 8, 128), f32),
+            pltpu.VMEM((6, 8, 8, 128), f32),
+            pltpu.VMEM((6, 7, 8, 128), f32),
             pltpu.VMEM((2, 64, 1024), f32),
             pltpu.VMEM((16, 8, DL), f32),
-            pltpu.VMEM((20, 5, 8, 128), f32),
+            pltpu.VMEM((24, 5, 8, 128), f32),
             pltpu.VMEM((16, 5, 8, 128), f32),
             dma,
+            dma((8,)),
             dma,
-            dma,
-            dma((16,)),
-            dma((16,)),
-            dma((16,)),
-            dma((16,)),
-            dma((16,)),
-            dma((20,)),
-            dma((20,)),
-            dma((5,)),
-            dma((5,)),
+            dma((16,)),
+            dma((16,)),
+            dma((16,)),
+            dma((16,)),
+            dma((16,)),
+            dma((21,)),
+            dma((21,)),
+            dma((6,)),
+            dma((6,)),
             dma((16,)),
             dma((16,)),
         ],

time: 43.7 us -> 40.5 us (0.927)
  Pallas kernels: 42.2 us -> 39 us
    pallas_call x1, Pallas kernels: 42.2 us -> 39 us  [local(): pl.pallas_call(kernel, out_shape=jax.ShapeDtypeStruct((4, 8, 128), bf16),...]
where the time goes in v3:
time: 40.5 us; the launch traced here: 40.3 us
  Pallas kernels  39 us (96%)
  local copies, waits for them, and re-layouts  1.3 us (3%)
    pallas_call x1, Pallas kernels, local(): pl.pallas_call(kernel, out_shape=jax.ShapeDtypeStruct((4, 8, 128), bf16),...  39 us
    unnamed x1, local copies, waits for them, and re-layouts  1.3 us

profile of v3, /device:TPU:1, one launch (start us, length us, event | category | flops | bytes accessed | tf_op | source)
XLA Modules:
  0.0 40.3 jit_solution(12072339518315831072)
XLA Ops:
  0.0 39.0 %shard_map.73 = bf16[4,8,128]{2,1,0:T(8,128)(2,1)} custom-call(s32[4]{0:T(128)} %bitcast.12, s32[16]{0:T(128)} %bitcast.13, s32[16]{0:T(128)} %bitcast.10, s32[1,16]{1,0:T(1,128)} %bitcast.11, bf16[4,64,576]{2,1,0:T(8,128)(2,1)} %queries_hbm.1, bf16[4,576,256]{2,1,0:T(8,128)(2,1)} %bitcast.9, bf16[16,576,1024]{2,1,0:T(8,128)(2,1)} %bitcast.8, ...), custom_call_target="tpu_custom_call" | custom-call | tf_op jit(solution)/shard_map/pallas_call | solution.py:379
  39.0 1.3 %copy.9 = bf16[4,8,128]{2,1,0:T(8,128)(2,1)} copy(bf16[4,8,128]{2,1,0:T(8,128)(2,1)} %shard_map.73) | data formatting | bytes 16384

commit v4 on v3

--- a/solution.py
+++ b/solution.py
@@ -67,6 +67,7 @@
     s_in,
     score_buffer,
     latent,
+    result,
     c_out,
     c_in,
     query_sem,
@@ -124,14 +125,13 @@
 
     def value_copy(h):
         half = value_up.at[h // 2, :, 128 * (h % 2) : 128 * (h % 2) + 128]
-        return pltpu.make_async_copy(value_hbm.at[h], half, value_sem.at[h])
+        return pltpu.make_async_copy(value_hbm.at[h], half, value_sem)
 
     for h in range(8):
         value_copy(h).start()
 
     def value_wait():
-        for h in range(8):
-            value_copy(h).wait()
+        pltpu.make_async_copy(value_up, value_up, value_sem).wait()
 
     o_out[4] = jnp.zeros((8, 8, DL), jnp.bfloat16)
     o_in[4] = jnp.zeros((7, 8, DL), jnp.bfloat16)
@@ -151,10 +151,10 @@
     lax.fori_loop(1, 16, select, 0)
 
     def plan_copy(k):
-        return remote(plan_v, plan_in.at[k], ps_sem.at[k], pr_sem.at[k], (ahead(k), sub))
+        return remote(plan_v, plan_in.at[k], ps_sem, pr_sem.at[k], (ahead(k), sub))
 
     def query_copy(k):
-        return remote(q_out.at[k], q_in.at[k], qs_sem.at[k], qr_sem.at[k], (ahead(k), sub))
+        return remote(q_out.at[k], q_in.at[k], qs_sem, qr_sem.at[k], (ahead(k), sub))
 
     pl.semaphore_wait(barrier, 22)
 
@@ -176,7 +176,7 @@
         for j in range(1, 8):
             to = peer(j)
             remote(
-                o_out.at[u, to], o_in.at[u, j - 1], os_sem.at[u], or_sem.at[u], (dp, to)
+                o_out.at[u, to], o_in.at[u, j - 1], os_sem, or_sem.at[u // 4], (dp, to)
             ).start()
 
     def send_stat(b):
@@ -184,7 +184,7 @@
         for j in range(1, 8):
             to = peer(j)
             remote(
-                s_out.at[b, to], s_in.at[b, j - 1], ss_sem.at[b], sr_sem.at[b], (dp, to)
+                s_out.at[b, to], s_in.at[b, j - 1], ss_sem, sr_sem.at[b], (dp, to)
             ).start()
         stat[...] = jnp.full((64, 128), masked_score, jnp.float32)
 
@@ -205,11 +205,8 @@
 
     def prepare(k):
         cache_copy(k).wait()
-
-        @pl.when(k > 0)
-        def _():
-            query_copy(k).wait_recv()
-            plan_copy(k).wait_recv()
+        query_copy(k).wait_recv()
+        plan_copy(k).wait_recv()
 
     def score_step(k):
         block = q_in[k]
@@ -235,19 +232,29 @@
         send_unit(k + 5)
 
     def c_copy(k):
-        return remote(c_out.at[k + 5], c_in.at[k], cs_sem.at[k], cr_sem.at[k], (behind(k), sub))
+        return remote(c_out.at[k + 5], c_in.at[k], cs_sem, cr_sem, (behind(k), sub))
 
     def combine(b, count=4):
         def all_in(buffer, target, semaphore):
             return pltpu.make_async_copy(buffer.at[pl.ds(0, 7)], target, semaphore)
 
         all_in(s_out.at[b], s_in.at[b], sr_sem.at[b]).wait()
-        for kk in range(count):
-            u = 4 * b + kk
-
-            @pl.when(u != 4)
+
+        def units_in(first, units):
+            block = o_in.at[pl.ds(first, units)]
+            pltpu.make_async_copy(block, block, or_sem.at[b]).wait()
+
+        if isinstance(b, int):
+            units_in(4 * b, count)
+        else:
+
+            @pl.when(b == 1)
             def _():
-                all_in(o_out.at[u], o_in.at[u], or_sem.at[u]).wait()
+                units_in(5, 3)
+
+            @pl.when(b != 1)
+            def _():
+                units_in(4 * b, 4)
 
         logs = [s_out[b, sub]] + [s_in[b, j] for j in range(7)]
         peak = logs[0]
@@ -292,6 +299,7 @@
     cache_copy(0).wait()
     score_buffer[0] = score_step(0)
     step(0, 0, True)
+    others = pl.ds(1, 15)
     for k in (1, 2):
         prepare(k)
         score_buffer[0] = score_step(k)
@@ -325,33 +333,15 @@
     combine(5, 1)
     send_back(5, 1)
 
-    def finish(k, carry):
-        query_copy(k).wait_send()
-        plan_copy(k).wait_send()
-        return carry
-
-    lax.fori_loop(1, 16, finish, 0)
-
-    def sent(u, carry):
-        @pl.when(u != 4)
-        def _():
-            pltpu.make_async_copy(o_out.at[u, pl.ds(0, 7)], o_in.at[u], os_sem.at[u]).wait()
-
-        return carry
-
-    lax.fori_loop(0, 21, sent, 0)
-
-    def sent_stat(b, carry):
-        pltpu.make_async_copy(s_out.at[b, pl.ds(0, 7)], s_in.at[b], ss_sem.at[b]).wait()
-        return carry
-
-    lax.fori_loop(0, 6, sent_stat, 0)
-
-    def arrive(k, carry):
-        c_copy(k).wait()
-        return carry
-
-    lax.fori_loop(1, 16, arrive, 0)
+    for block, semaphore in (
+        (q_in.at[others], qs_sem),
+        (plan_in.at[others], ps_sem),
+        (o_in.at[pl.ds(0, 20)], os_sem),
+        (s_in, ss_sem),
+        (c_in.at[others], cs_sem),
+        (c_in.at[others], cr_sem),
+    ):
+        pltpu.make_async_copy(block, block, semaphore).wait()
 
     parts = [c_out.at[u] for u in (0, 1, 2, 3, 5)] + [c_in.at[k] for k in range(1, 16)]
     peak = parts[0][4]
@@ -365,7 +355,10 @@
         for r in range(4):
             sums[r] = sums[r] + weight[:, r : r + 1] * part[r]
     for r in range(4):
-        out[r] = (sums[r] / total[:, r : r + 1]).astype(out.dtype)
+        result[r] = (sums[r] / total[:, r : r + 1]).astype(out.dtype)
+    out_copy = pltpu.make_async_copy(result, out, query_sem)
+    out_copy.start()
+    out_copy.wait()
 
 
 def local(queries, own_cache, own_len, host_cache, host_len, page_plan, value_up):
@@ -380,7 +373,7 @@
         kernel,
         out_shape=jax.ShapeDtypeStruct((4, 8, 128), bf16),
         in_specs=[smem, smem, smem, vmem, anywhere, anywhere, anywhere, anywhere],
-        out_specs=vmem,
+        out_specs=anywhere,
         scratch_shapes=[
             pltpu.VMEM((4, 64, 576), bf16),
             pltpu.VMEM((4, DL, 256), bf16),
@@ -397,22 +390,23 @@
             pltpu.VMEM((6, 7, 8, 128), f32),
             pltpu.VMEM((2, 64, 1024), f32),
             pltpu.VMEM((16, 8, DL), f32),
+            pltpu.VMEM((4, 8, 128), bf16),
             pltpu.VMEM((24, 5, 8, 128), f32),
             pltpu.VMEM((16, 5, 8, 128), f32),
             dma,
-            dma((8,)),
+            dma,
             dma,
             dma((16,)),
+            dma,
             dma((16,)),
+            dma,
             dma((16,)),
-            dma((16,)),
-            dma((16,)),
-            dma((21,)),
-            dma((21,)),
+            dma,
             dma((6,)),
+            dma,
             dma((6,)),
-            dma((16,)),
-            dma((16,)),
+            dma,
+            dma,
         ],
         compiler_params=pltpu.CompilerParams(
             vmem_limit_bytes=60 * 2**20, collective_id=0, has_side_effects=True

time: 40.5 us -> 39.5 us (0.975)
  Pallas kernels: 39 us -> 38.1 us
    pallas_call x1, Pallas kernels: 39 us -> 38.1 us  [local(): pl.pallas_call(kernel, out_shape=jax.ShapeDtypeStruct((4, 8, 128), bf16),...]
where the time goes in v4:
time: 39.5 us; the launch traced here: 39.4 us
  Pallas kernels  38.1 us (96%)
  local copies, waits for them, and re-layouts  1.3 us (3%)
    pallas_call x1, Pallas kernels, local(): pl.pallas_call(kernel, out_shape=jax.ShapeDtypeStruct((4, 8, 128), bf16),...  38.1 us
    unnamed x1, local copies, waits for them, and re-layouts  1.3 us

profile of v4, /device:TPU:1, one launch (start us, length us, event | category | flops | bytes accessed | tf_op | source)
XLA Modules:
  0.0 39.4 jit_solution(14160274363456479503)
XLA Ops:
  0.0 38.1 %shard_map.73 = bf16[4,8,128]{2,1,0:T(8,128)(2,1)} custom-call(s32[4]{0:T(128)} %bitcast.12, s32[16]{0:T(128)} %bitcast.13, s32[16]{0:T(128)} %bitcast.10, s32[1,16]{1,0:T(1,128)} %bitcast.11, bf16[4,64,576]{2,1,0:T(8,128)(2,1)} %queries_hbm.1, bf16[4,576,256]{2,1,0:T(8,128)(2,1)} %bitcast.9, bf16[16,576,1024]{2,1,0:T(8,128)(2,1)} %bitcast.8, ...), custom_call_target="tpu_custom_call" | custom-call | tf_op jit(solution)/shard_map/pallas_call | solution.py:372
  38.1 1.3 %copy.9 = bf16[4,8,128]{2,1,0:T(8,128)(2,1)} copy(bf16[4,8,128]{2,1,0:T(8,128)(2,1)} %shard_map.73) | data formatting | bytes 16384

commit v5 on v4

--- a/solution.py
+++ b/solution.py
@@ -173,7 +173,7 @@
     plan_in[0] = plan_v[...]
 
     def send_unit(u):
-        for j in range(1, 8):
+        for j in (4, 5, 3, 2, 6, 7, 1):
             to = peer(j)
             remote(
                 o_out.at[u, to], o_in.at[u, j - 1], os_sem, or_sem.at[u // 4], (dp, to)
@@ -181,7 +181,7 @@
 
     def send_stat(b):
         s_out[b] = stat[...].reshape(8, 8, 128)
-        for j in range(1, 8):
+        for j in (4, 5, 3, 2, 6, 7, 1):
             to = peer(j)
             remote(
                 s_out.at[b, to], s_in.at[b, j - 1], ss_sem, sr_sem.at[b], (dp, to)
@@ -200,7 +200,8 @@
         send_unit(r)
         return carry
 
-    lax.fori_loop(0, 4, own_step, 0)
+    for r in range(4):
+        own_step(r, 0)
     send_stat(0)
 
     def prepare(k):

time: 39.5 us -> 39.4 us (level)
  no operation moved by 1% of the time
where the time goes in v5:
time: 39.4 us; the launch traced here: 39.3 us
  Pallas kernels  38 us (96%)
  local copies, waits for them, and re-layouts  1.3 us (3%)
    pallas_call x1, Pallas kernels, local(): pl.pallas_call(kernel, out_shape=jax.ShapeDtypeStruct((4, 8, 128), bf16),...  38 us
    unnamed x1, local copies, waits for them, and re-layouts  1.3 us

profile of v5, /device:TPU:1, one launch (start us, length us, event | category | flops | bytes accessed | tf_op | source)
XLA Modules:
  0.0 39.3 jit_solution(10208498200917184032)
XLA Ops:
  0.0 38.0 %shard_map.73 = bf16[4,8,128]{2,1,0:T(8,128)(2,1)} custom-call(s32[4]{0:T(128)} %bitcast.12, s32[16]{0:T(128)} %bitcast.13, s32[16]{0:T(128)} %bitcast.10, s32[1,16]{1,0:T(1,128)} %bitcast.11, bf16[4,64,576]{2,1,0:T(8,128)(2,1)} %queries_hbm.1, bf16[4,576,256]{2,1,0:T(8,128)(2,1)} %bitcast.9, bf16[16,576,1024]{2,1,0:T(8,128)(2,1)} %bitcast.8, ...), custom_call_target="tpu_custom_call" | custom-call | tf_op jit(solution)/shard_map/pallas_call | solution.py:373
  38.0 1.3 %copy.9 = bf16[4,8,128]{2,1,0:T(8,128)(2,1)} copy(bf16[4,8,128]{2,1,0:T(8,128)(2,1)} %shard_map.73) | data formatting | bytes 16384
